TPU v7x, 32 devices: a whole 2x2x4 slice. The times are simulated.
32 devices in a mesh: tok: 16 (over z, y, x), hd: 2 (over core).
Axes of the slice: x: 2, y: 2, z: 4, core: 2. Of those that a mesh axis runs over, the one named last changes fastest.
Arguments:
- hidden_in: bfloat16 [16384, 768], P(('tok', 'hd')), may hold values from -6 to 6
- norm_gains: bfloat16 [2, 768], P(None, ('tok', 'hd')), may hold values from 0.099609375 to 1.8984375
- w_qkv: bfloat16 [2304, 768], P(('tok', 'hd')), may hold values from -0.21875 to 0.21875
- w_attn_out: bfloat16 [768, 768], P(('tok', 'hd')), may hold values from -1.75 to 1.75
- w_in: bfloat16 [2304, 768], P(('tok', 'hd')), may hold values from -0.21875 to 0.21875
- w_down: bfloat16 [768, 1152], P(('tok', 'hd')), may hold values from -0.1875 to 0.1875
- cotangent: bfloat16 [16384, 768], P(('tok', 'hd')), may hold values from -6 to 6
- segment_ids: int32 [16384], P(('tok', 'hd')), may hold values from 0 to 31, as said below
- row_counts: int32 [32], P(('tok', 'hd')), may hold values from 256 to 512, as said below
Outputs:
- output: bfloat16 [16384, 768], P(('tok', 'hd'))
- input_grad: bfloat16 [16384, 768], P(('tok', 'hd'))
- grad_qkv: float32 [2304, 768], P(('tok', 'hd'))
- grad_attn_out: float32 [768, 768], P(('tok', 'hd'))
- grad_in: float32 [2304, 768], P(('tok', 'hd'))
- grad_down: float32 [768, 1152], P(('tok', 'hd'))
- grad_gains: float32 [2, 768], P(None, ('tok', 'hd'))
Inputs may be any that keep to these rules, and one draw needn't show every extreme that they name: `segment_ids`: within each group of 1024 rows the ids start at 0 and never fall; a document is a run of rows with one id; documents begin only at rows whose index within the group is a multiple of 32, and always at rows whose index within a block is 256, so a document may span two blocks of a group. In every draw some group holds 32 documents. `row_counts`: rows of a block at or beyond its count are padding.
All inputs are finite; a program needn't handle non-finite values.
Results may differ from a plain program's by a relative error of at most 0.015.
Values may be sent and summed in bfloat16 or wider, within the bound.
A program may use at most 192 MiB of HBM per device.

v0:
```python
import math

import jax
import jax.numpy as jnp
from jax import lax
from jax.sharding import PartitionSpec as P

HEADS = 12
HEAD_DIM = 64


EPS = 1e-05
THETA = 160000.0
NEG = -1e30


def layer_norm(row_values, gain):
    mean_value = jnp.mean(row_values, axis=-1, keepdims=True)
    centred = row_values - mean_value
    variance = jnp.mean(centred * centred, axis=-1, keepdims=True)
    return centred * lax.rsqrt(variance + EPS) * gain


def doc_positions(seg_ids):
    row_index = jnp.arange(seg_ids.shape[0], dtype=jnp.int32)
    begins = jnp.concatenate([jnp.ones((1,), dtype=jnp.bool_), seg_ids[1:] != seg_ids[:-1]])
    first_row = lax.cummax(jnp.where(begins, row_index, 0), axis=0)
    return (row_index - first_row).astype(jnp.float32)


def rotary_tables(position, head_size):
    half_size = head_size // 2
    freqs = THETA ** (-jnp.arange(half_size, dtype=jnp.float32) * 2.0 / head_size)
    angles = position[:, None] * freqs[None, :]
    angles = jnp.concatenate([angles, angles], axis=1)
    return (jnp.cos(angles), jnp.sin(angles))


def rotate(head_values, cos_table, sin_table):
    half_size = head_values.shape[-1] // 2
    turned = jnp.concatenate([-head_values[..., half_size:], head_values[..., :half_size]], axis=-1)
    return head_values * cos_table[:, None, :] + turned * sin_table[:, None, :]


def times_t(left, right):
    return lax.dot_general(
        left, right, (((1,), (1,)), ((), ())), preferred_element_type=jnp.float32
    )


def outer_sum(left, right):
    return lax.dot_general(
        left, right, (((0,), (0,)), ((), ())), preferred_element_type=jnp.float32
    )


def times(left, right):
    return jnp.dot(left, right, preferred_element_type=jnp.float32)


def gated(gate, up_part):
    return jax.nn.gelu(gate, approximate=False) * up_part


def block_scores(queries, keys, seg_ids, ok_rows, first_row, block_size):
    query_block = lax.dynamic_slice_in_dim(queries, first_row, block_size, 0)
    seg_query = lax.dynamic_slice_in_dim(seg_ids, first_row, block_size, 0)
    ok_query = lax.dynamic_slice_in_dim(ok_rows, first_row, block_size, 0)
    query_index = first_row + jnp.arange(block_size, dtype=jnp.int32)
    key_index = jnp.arange(seg_ids.shape[0], dtype=jnp.int32)
    same_doc = (seg_query[:, None] == seg_ids[None, :]) & ok_query[:, None] & ok_rows[None, :]
    allowed = same_doc | (query_index[:, None] == key_index[None, :])
    scores = (
        jnp.einsum("qhd,khd->hqk", query_block, keys, preferred_element_type=jnp.float32) * 0.125
    )
    return (query_block, allowed, jnp.where(allowed[None], scores, NEG))


def attend_forward(queries, keys, values, seg_ids, ok_rows, block_size):

    def one_block(block_index):
        first_row = block_index * block_size
        _, _, masked = block_scores(queries, keys, seg_ids, ok_rows, first_row, block_size)
        top_score = jnp.max(masked, axis=-1, keepdims=True)
        weights_exp = jnp.exp(masked - top_score)
        total = jnp.sum(weights_exp, axis=-1, keepdims=True)
        probs = (weights_exp / total).astype(jnp.bfloat16)
        mixed = jnp.einsum("hqk,khd->qhd", probs, values, preferred_element_type=jnp.float32)
        return (mixed.astype(jnp.bfloat16), (top_score + jnp.log(total))[..., 0])

    block_ids = jnp.arange(queries.shape[0] // block_size, dtype=jnp.int32)
    mixed, log_totals = lax.map(one_block, block_ids)
    return (mixed.reshape(queries.shape), log_totals)


def attend_backward(queries, keys, values, grad_mixed, log_totals, seg_ids, ok_rows, block_size):

    def one_block(carry, inputs_here):
        grad_keys, grad_values = carry
        block_index, log_total = inputs_here
        first_row = block_index * block_size
        query_block, allowed, masked = block_scores(
            queries, keys, seg_ids, ok_rows, first_row, block_size
        )
        probs = jnp.exp(masked - log_total[..., None])
        probs_low = probs.astype(jnp.bfloat16)
        grad_block = lax.dynamic_slice_in_dim(grad_mixed, first_row, block_size, 0)
        grad_probs = jnp.einsum(
            "qhd,khd->hqk", grad_block, values, preferred_element_type=jnp.float32
        )
        inner = jnp.sum(probs * grad_probs, axis=-1, keepdims=True)
        grad_scores = jnp.where(allowed[None], probs * (grad_probs - inner), 0.0).astype(
            jnp.bfloat16
        )
        grad_query = (
            jnp.einsum("hqk,khd->qhd", grad_scores, keys, preferred_element_type=jnp.float32)
            * 0.125
        )
        grad_keys = (
            grad_keys
            + jnp.einsum(
                "hqk,qhd->khd", grad_scores, query_block, preferred_element_type=jnp.float32
            )
            * 0.125
        )
        grad_values = grad_values + jnp.einsum(
            "hqk,qhd->khd", probs_low, grad_block, preferred_element_type=jnp.float32
        )
        return ((grad_keys, grad_values), grad_query.astype(jnp.bfloat16))

    zero_grads = jnp.zeros(keys.shape, jnp.float32)
    block_ids = jnp.arange(queries.shape[0] // block_size, dtype=jnp.int32)
    (grad_keys, grad_values), grad_query = lax.scan(
        one_block, (zero_grads, zero_grads), (block_ids, log_totals)
    )
    return (
        grad_query.reshape(queries.shape),
        grad_keys.astype(jnp.bfloat16),
        grad_values.astype(jnp.bfloat16),
    )


def per_device(
    hidden_in, norm_gains, w_qkv, w_attn_out, w_in, w_down, cotangent, segment_ids, row_counts
):
    row_total, width = hidden_in.shape
    group_count = lax.axis_size("hd")
    heads_here = HEADS // group_count
    part_width = width // group_count
    group_rows = group_count * row_total
    block_size = min(512, group_rows)
    ff_width = w_down.shape[1]
    gathered = (
        lax.all_gather(w_qkv, ("tok", "hd"), axis=0, tiled=True),
        lax.all_gather(w_attn_out, ("tok", "hd"), axis=0, tiled=True),
        lax.all_gather(w_in, ("tok", "hd"), axis=0, tiled=True),
        lax.all_gather(w_down, ("tok", "hd"), axis=0, tiled=True),
        lax.all_gather(norm_gains, ("tok", "hd"), axis=1, tiled=True),
    )
    full_qkv, full_attn_out, full_in, full_down, full_gains = gathered
    gain_attn = full_gains[0].astype(jnp.float32)
    gain_mlp = full_gains[1].astype(jnp.float32)
    row_index = jnp.arange(row_total, dtype=jnp.int32)
    keep_rows = (row_index < row_counts[0]).astype(jnp.float32)[:, None]
    seg_pair, count_pair = (
        lax.all_gather(segment_ids, "hd", axis=0, tiled=True),
        lax.all_gather(row_counts, "hd", axis=0, tiled=True),
    )
    ok_pair = jnp.concatenate([row_index < count_pair[anchor] for anchor in range(group_count)])
    group_positions = doc_positions(seg_pair)
    own_start = lax.axis_index("hd") * row_total
    own_positions = lax.dynamic_slice_in_dim(group_positions, own_start, row_total, 0)
    cos_table, sin_table = rotary_tables(own_positions, HEAD_DIM)
    wide_in = hidden_in.astype(jnp.float32)
    normed_f, attn_norm_pull = jax.vjp(layer_norm, wide_in, gain_attn)
    normed1 = normed_f.astype(jnp.bfloat16)
    qkv = times_t(normed1, full_qkv)
    q_rot = rotate(qkv[:, :width].reshape(row_total, HEADS, HEAD_DIM), cos_table, sin_table)
    k_rot = rotate(
        qkv[:, width : 2 * width].reshape(row_total, HEADS, HEAD_DIM), cos_table, sin_table
    )
    packed = jnp.concatenate(
        [q_rot.reshape(row_total, width), k_rot.reshape(row_total, width), qkv[:, 2 * width :]],
        axis=1,
    ).astype(jnp.bfloat16)
    packed = packed.reshape(row_total, 3, group_count, part_width)
    head_rows = lax.all_to_all(packed, "hd", split_axis=2, concat_axis=0, tiled=True)
    q_heads = head_rows[:, 0, 0].reshape(group_rows, heads_here, HEAD_DIM)
    k_heads = head_rows[:, 1, 0].reshape(group_rows, heads_here, HEAD_DIM)
    v_heads = head_rows[:, 2, 0].reshape(group_rows, heads_here, HEAD_DIM)
    mixed, log_totals = attend_forward(q_heads, k_heads, v_heads, seg_pair, ok_pair, block_size)
    mixed_heads = mixed.reshape(group_rows, 1, part_width)
    attended = lax.all_to_all(mixed_heads, "hd", split_axis=0, concat_axis=1, tiled=True).reshape(
        row_total, width
    )
    residual = wide_in + keep_rows * times_t(attended, full_attn_out)
    normed_g, mlp_norm_pull = jax.vjp(layer_norm, residual, gain_mlp)
    normed2 = normed_g.astype(jnp.bfloat16)
    both_parts = times_t(normed2, full_in)
    hidden_f, gate_pull = jax.vjp(gated, both_parts[:, :ff_width], both_parts[:, ff_width:])
    hidden = hidden_f.astype(jnp.bfloat16)
    output = (residual + keep_rows * times_t(hidden, full_down)).astype(jnp.bfloat16)
    back_weights = (
        lax.all_gather(w_qkv, ("tok", "hd"), axis=0, tiled=True),
        lax.all_gather(w_attn_out, ("tok", "hd"), axis=0, tiled=True),
        lax.all_gather(w_in, ("tok", "hd"), axis=0, tiled=True),
        lax.all_gather(w_down, ("tok", "hd"), axis=0, tiled=True),
        lax.all_gather(norm_gains, ("tok", "hd"), axis=1, tiled=True),
    )
    back_qkv, back_attn_out, back_in, back_down, _ = back_weights
    grad_out_rows = cotangent.astype(jnp.float32)
    grad_branch2 = (keep_rows * grad_out_rows).astype(jnp.bfloat16)
    down_term = outer_sum(grad_branch2, hidden)
    grad_hidden = times(grad_branch2, back_down)
    grad_gate, grad_up = gate_pull(grad_hidden)
    grad_both = jnp.concatenate([grad_gate, grad_up], axis=1).astype(jnp.bfloat16)
    in_term = outer_sum(grad_both, normed2)
    grad_normed2 = times(grad_both, back_in)
    grad_res_norm, gain_mlp_term = mlp_norm_pull(grad_normed2)
    grad_residual = grad_out_rows + grad_res_norm
    grad_branch1 = (keep_rows * grad_residual).astype(jnp.bfloat16)
    attn_out_term = outer_sum(grad_branch1, attended)
    grad_attended = times(grad_branch1, back_attn_out).astype(jnp.bfloat16)
    grad_heads = lax.all_to_all(
        grad_attended.reshape(row_total, group_count, part_width),
        "hd",
        split_axis=1,
        concat_axis=0,
        tiled=True,
    )
    grad_heads = grad_heads.reshape(group_rows, heads_here, HEAD_DIM)
    grad_query, grad_keys, grad_values = attend_backward(
        q_heads, k_heads, v_heads, grad_heads, log_totals, seg_pair, ok_pair, block_size
    )
    grad_stack = jnp.stack(
        [
            grad_query.reshape(group_rows, part_width),
            grad_keys.reshape(group_rows, part_width),
            grad_values.reshape(group_rows, part_width),
        ],
        axis=1,
    )
    grad_stack = grad_stack.reshape(group_rows, 3, 1, part_width)
    grad_rows = lax.all_to_all(grad_stack, "hd", split_axis=0, concat_axis=2, tiled=True).reshape(
        row_total, 3, width
    )
    grad_q = rotate(
        grad_rows[:, 0].astype(jnp.float32).reshape(row_total, HEADS, HEAD_DIM),
        cos_table,
        -sin_table,
    )
    grad_k = rotate(
        grad_rows[:, 1].astype(jnp.float32).reshape(row_total, HEADS, HEAD_DIM),
        cos_table,
        -sin_table,
    )
    grad_qkv = jnp.concatenate(
        [
            grad_q.reshape(row_total, width).astype(jnp.bfloat16),
            grad_k.reshape(row_total, width).astype(jnp.bfloat16),
            grad_rows[:, 2],
        ],
        axis=1,
    )
    qkv_term = outer_sum(grad_qkv, normed1)
    grad_normed1 = times(grad_qkv, back_qkv)
    grad_in_norm, gain_attn_term = attn_norm_pull(grad_normed1)
    input_grad = (grad_residual + grad_in_norm).astype(jnp.bfloat16)
    gain_terms = jnp.stack([gain_attn_term, gain_mlp_term])
    sum_qkv, sum_attn_out, sum_in, sum_down, sum_gains = (
        lax.psum_scatter(qkv_term, ("tok", "hd"), scatter_dimension=0, tiled=True),
        lax.psum_scatter(attn_out_term, ("tok", "hd"), scatter_dimension=0, tiled=True),
        lax.psum_scatter(in_term, ("tok", "hd"), scatter_dimension=0, tiled=True),
        lax.psum_scatter(down_term, ("tok", "hd"), scatter_dimension=0, tiled=True),
        lax.psum_scatter(gain_terms, ("tok", "hd"), scatter_dimension=1, tiled=True),
    )
    token_total = row_total * lax.axis_size("tok") * lax.axis_size("hd")
    scale = 1.0 / math.sqrt(token_total)
    return (
        output,
        input_grad,
        sum_qkv * scale,
        sum_attn_out * scale,
        sum_in * scale,
        sum_down * scale,
        sum_gains * scale,
    )


def solution(mesh):
    return jax.shard_map(
        per_device,
        mesh=mesh,
        in_specs=(
            P(("tok", "hd"), None),
            P(None, ("tok", "hd")),
            P(("tok", "hd"), None),
            P(("tok", "hd"), None),
            P(("tok", "hd"), None),
            P(("tok", "hd"), None),
            P(("tok", "hd"), None),
            P(("tok", "hd")),
            P(("tok", "hd")),
        ),
        out_specs=(
            P(("tok", "hd"), None),
            P(("tok", "hd"), None),
            P(("tok", "hd"), None),
            P(("tok", "hd"), None),
            P(("tok", "hd"), None),
            P(("tok", "hd"), None),
            P(None, ("tok", "hd")),
        ),
        check_vma=False,
    )
```

profile of v0, /device:TPU:0, one launch (start us, length us, event | category | flops | bytes accessed | tf_op | source)
XLA Modules:
  0.0 732.9 jit_solution(1573320555635671999)
XLA Ops:
  21.4 43.4 %all-gather.1 = bf16[32,24,2]{1,2,0:T(2,128)(2,1)S(1)} all-gather(bf16[1,24,2]{1,2,0:T(2,128)(2,1)} %bitcast.176), channel_id=1, replica_groups=mesh['tok'=16,'hd'=2] {'tok','hd'}, dimensions={0}, use_global_device_ids=true | all-gather | bytes 3168 | tf_op jit(solution)/shard_map/all_gather | solution.py:158
  71.1 2.6 all-gather.7.cloned.1.call-done
  73.7 4.1 fusion.125
  82.1 3.0 copy.85
  85.1 3.0 copy.88
  88.2 2.3 slice_negate_fusion.2
  92.7 3.1 copy.86
  95.8 3.0 copy.89
  98.8 4.2 add_convert_fusion.4
  105.9 5.8 all_to_all.63
  113.1 25.3 %while.27 = (s32[]{:T(128)}, bf16[2,512,6,64]{1,3,2,0:T(8,128)(2,1)S(1)}, f32[2,6,512]{2,1,0:T(8,128)S(1)}, s32[2]{0:T(128)S(1)}, s32[1024]{0:T(1024)S(1)}, /*in...) while((s32[]{:T(128)}, ...), condition=%wide.region_7.8_spmd, body=%wide.region_4.7_spmd.sunk | while | flops 845870592 | bytes 42341076 | solution.py:92
  115.2 2.4 fusion.178
  117.6 3.6 fusion.179
  121.3 4.4 fusion.180
  127.9 2.4 fusion.178
  130.3 3.6 fusion.179
  133.9 4.4 fusion.180
  140.1 2.5 reshape_reshape.3
  147.5 5.8 all_to_all.64
  155.0 2.5 copy.108
  159.8 2.5 fusion.134
  163.8 27.4 %all-gather.11.cloned.1.call-done = bf16[2304,768]{1,0:T(8,128)(2,1)} async-done(((bf16[72,768]{1,0:T(8,128)(2,1)}), bf16[2304,768]{1,0:T(8,128)(2,1)}) %all-gather.11.cloned.1.call-update) | async-done | bytes 3538960 | tf_op jit(solution)/shard_map/all_gather | solution.py:156
  191.2 6.8 fusion.128
  197.9 50.2 %all-gather.13.cloned.1.call-done = bf16[768,1152]{1,0:T(8,128)(2,1)} async-done(((bf16[24,1152]{1,0:T(8,128)(2,1)}), bf16[768,1152]{1,0:T(8,128)(2,1)}) %all-gather.13.cloned.1.call-update) | async-done | bytes 1769488 | tf_op jit(solution)/shard_map/all_gather | solution.py:157
  248.1 9.0 %add_convert_fusion = (bf16[512,1152]{1,0:T(8,128)(2,1)S(1)}, f32[512,1152]{1,0:T(8,128)S(1)}, f32[512,1152]{1,0:T(8,128)S(1)}) fusion(f32[512,2304]{1,0:T(8,128)} %fusion.128, bf16[768,1152]{1,0:T(8,128)(2,1)} %all-gather.13.cloned.1.call-done, bf16[512,768]{1,0:T(8,128)(2,1)S(1)} %copy-done.8, f32[512]{0:T(512)S(1)} %copy-done.32), kind=kOutput, calls=%fused_computation.82 | convolution fusion | flops 950206464 | bytes 13174784 | tf_op jit(solution)/shard_map/dot_general | solution.py:58
  260.9 2.7 multiply_reduce_fusion.1
  268.9 4.3 fusion.107
  273.3 7.2 fusion.103
  283.8 4.4 all_to_all.65
  290.1 3.2 reshape.416
  294.3 145.9 %while.28 = (s32[]{:T(128)}, f32[1024,6,64]{0,2,1:T(8,128)}, f32[1024,6,64]{0,2,1:T(8,128)}, bf16[2,512,6,64]{1,3,2,0:T(8,128)(2,1)}, s32[2]{0:T(128)S(1)}, /*in...) while((s32[]{:T(128)}, f32[1024,6,64]{0,2,1:T(8,128)}, ...), condition=%wide.region_14.15_spmd.clone, body=%wide.region_12.14_spmd.clone.sunk | while | flops 2100044288 | bytes 205775664 | solution.py:133
  298.3 5.0 bitcast_add_fusion.7
  303.3 6.3 fusion.191
  309.6 27.1 %fusion.194 = bf16[2,512,6,64]{1,3,2,0:T(8,128)(2,1)} fusion(bf16[2,512,6,64]{1,3,2,0:T(8,128)(2,1)} %get-tuple-element.481, s32[]{:T(128)S(6)} %copy.130, bf16[1024,6,64]{0,2,1:T(8,128)(2,1)S(1)} %get-tuple-element.502, f32[6,512,1024]{2,1,0:T(8,128)} %fusion.191, f32[6,512,1024]{2,1,0:T(8,128)} %copy-done, ...), kind=kOutput, calls=%fused_computation.45.clone.1 | convolution fusion | flops 437653504 | bytes 52592644 | tf_op jit(solution)/shard_map/while/body/eval_jaxpr/hqk,khd->qhd/dot_general | solution.py:116
  336.7 29.5 %bitcast_add_fusion.6 = f32[1024,6,64]{0,2,1:T(8,128)} fusion(f32[1024,6,64]{0,2,1:T(8,128)} %get-tuple-element.479, f32[6,512,1024]{2,1,0:T(8,128)} %fusion.191, f32[6,512,1024]{2,1,0:T(8,128)} %copy-done, f32[6,512]{1,0:T(8,128)S(1)} %dynamic-slice_bitcast_fusion.2, pred[512,1024]{1,0:T(8,128)(4,1)S(1)} %fusion.193, pred[]{:T(512)S(6)} %compare.3, ...), kind=kOutput, calls=%fused_computation.41.clone.1 | convolution fusion | flops 438439936 | bytes 54951940 | tf_op jit(solution)/shard_map/while/body/eval_jaxpr/hqk,qhd->khd/dot_general | solution.py:121
  370.1 6.5 bitcast_add_fusion.7
  376.6 6.3 fusion.191
  382.9 27.3 %fusion.194 = bf16[2,512,6,64]{1,3,2,0:T(8,128)(2,1)} fusion(bf16[2,512,6,64]{1,3,2,0:T(8,128)(2,1)} %get-tuple-element.481, s32[]{:T(128)S(6)} %copy.130, bf16[1024,6,64]{0,2,1:T(8,128)(2,1)S(1)} %get-tuple-element.502, f32[6,512,1024]{2,1,0:T(8,128)} %fusion.191, f32[6,512,1024]{2,1,0:T(8,128)} %copy-done, ...), kind=kOutput, calls=%fused_computation.45.clone.1 | convolution fusion | flops 437653504 | bytes 52592644 | tf_op jit(solution)/shard_map/while/body/eval_jaxpr/hqk,khd->qhd/dot_general | solution.py:116
  410.2 29.8 %bitcast_add_fusion.6 = f32[1024,6,64]{0,2,1:T(8,128)} fusion(f32[1024,6,64]{0,2,1:T(8,128)} %get-tuple-element.479, f32[6,512,1024]{2,1,0:T(8,128)} %fusion.191, f32[6,512,1024]{2,1,0:T(8,128)} %copy-done, f32[6,512]{1,0:T(8,128)S(1)} %dynamic-slice_bitcast_fusion.2, pred[512,1024]{1,0:T(8,128)(4,1)S(1)} %fusion.193, pred[]{:T(512)S(6)} %compare.3, ...), kind=kOutput, calls=%fused_computation.41.clone.1 | convolution fusion | flops 438439936 | bytes 54951940 | tf_op jit(solution)/shard_map/while/body/eval_jaxpr/hqk,qhd->khd/dot_general | solution.py:121
  446.2 4.9 copy.103
  451.1 6.3 all_to_all.66
  459.1 2.8 copy.105
  466.3 5.1 fusion.105
  473.0 4.2 fusion.100
  479.3 38.3 %all-reduce.2 = f32[2,768]{1,0:T(2,128)S(1)} all-reduce(f32[2,768]{1,0:T(2,128)S(1)} %pad_maximum_fusion.8), channel_id=6, replica_groups=mesh['tok'=16,'hd'=2] {'tok','hd'}, use_global_device_ids=true, to_apply=%region_23.24.clone | all-reduce | flops 1536 | bytes 12288
  518.3 3.2 add_convert_fusion.1
  526.7 73.3 %reduce-scatter.12.cloned.1.call-done = f32[72,768]{1,0:T(8,128)} async-done(((f32[2304,768]{1,0:T(8,128)}), f32[72,768]{1,0:T(8,128)}) %reduce-scatter.12.cloned.1.call-update) | async-done | bytes 221200 | tf_op jit(solution)/shard_map/reduce_scatter | solution.py:273
  601.6 122.6 %reduce-scatter.8.cloned.1.call-done = f32[72,768]{1,0:T(8,128)} async-done(((f32[2304,768]{1,0:T(8,128)}), f32[72,768]{1,0:T(8,128)}) %reduce-scatter.8.cloned.1.call-update) | async-done | bytes 221200 | tf_op jit(solution)/shard_map/reduce_scatter | solution.py:271
  (236 shorter events, 91.6 us)
Async XLA Ops:
  7.2 66.5 %all-gather.7.cloned.1.call-start = ((), (), s32[]{:S(2)}) async-start(), calls=%async_computation.8 | async-start | bytes 3649536 | tf_op jit(solution)/shard_map/all_gather | solution.py:154
  7.9 151.9 %all-gather.9.cloned.1.call-start = ((), (), s32[]{:S(2)}) async-start(), calls=%async_computation.9 | async-start | bytes 1216512 | tf_op jit(solution)/shard_map/all_gather | solution.py:155
  8.6 182.5 %all-gather.11.cloned.1.call-start = ((), (), s32[]{:S(2)}) async-start(), calls=%async_computation.10 | async-start | bytes 3649536 | tf_op jit(solution)/shard_map/all_gather | solution.py:156
  9.4 238.7 %all-gather.13.cloned.1.call-start = ((), (), s32[]{:S(2)}) async-start(), calls=%async_computation.11 | async-start | bytes 1824768 | tf_op jit(solution)/shard_map/all_gather | solution.py:157
  10.0 513.7 %reduce-scatter.10.cloned.1.call-start = ((), (), s32[]{:S(2)}) async-start(), calls=%async_computation.13 | async-start | bytes 2433024 | tf_op jit(solution)/shard_map/reduce_scatter | solution.py:272
  17.1 56.6 %copy-start.34 = (f32[512]{0:T(512)}, f32[512]{0:T(512)S(1)}, u32[]{:S(2)}) copy-start(f32[512]{0:T(512)S(1)} %broadcast_multiply_fusion.6) | copy-start | bytes 6148
  18.6 51.2 %copy-start.40 = (f32[512]{0:T(512)}, f32[512]{0:T(512)S(1)}, u32[]{:S(2)}) copy-start(f32[512]{0:T(512)S(1)} %fusion.99) | copy-start | bytes 6148
  18.6 55.0 %copy-start.36 = (f32[512]{0:T(512)}, f32[512]{0:T(512)S(1)}, u32[]{:S(2)}) copy-start(f32[512]{0:T(512)S(1)} %fusion.118) | copy-start | bytes 6148
  65.5 8.2 %copy-start.30 = (f32[768]{0:T(1024)}, f32[768]{0:T(1024)S(1)}, u32[]{:S(2)}) copy-start(f32[768]{0:T(1024)S(1)} %get-tuple-element.201) | copy-start | bytes 9220
  66.5 1.4 copy-start.21
  66.5 7.2 copy-start.3
  77.8 2.1 copy-start.6
  155.0 4.8 copy-start.4
  155.0 4.8 copy-start.32
  159.8 31.4 %copy-start.42 = (f32[768]{0:T(1024)S(1)}, f32[768]{0:T(1024)}, u32[]{:S(2)}) copy-start(f32[768]{0:T(1024)} %get-tuple-element.200) | copy-start | bytes 9220
  191.1 57.0 %copy-start.8 = (bf16[512,768]{1,0:T(8,128)(2,1)S(1)}, bf16[512,768]{1,0:T(8,128)(2,1)}, u32[]{:S(2)}) copy-start(bf16[512,768]{1,0:T(8,128)(2,1)} %param.19) | copy-start | bytes 2359300
  248.1 9.0 %copy-start.15 = (f32[512,2304]{1,0:T(8,128)S(1)}, f32[512,2304]{1,0:T(8,128)}, u32[]{:S(2)}) copy-start(f32[512,2304]{1,0:T(8,128)} %fusion.128) | copy-start | bytes 14155780
  257.1 1.6 copy-start.46
  257.1 2.3 copy-start.11
  257.1 3.7 copy-start.44
  258.7 4.9 copy-start.20
  264.2 2.4 copy-start.16
  264.3 1.4 copy-start.38
  268.8 256.3 %reduce-scatter.14.cloned.1.call-start = ((), (), s32[]{:S(2)}) async-start(), calls=%async_computation.15 | async-start | bytes 3649536
  273.2 326.7 %reduce-scatter.12.cloned.1.call-start = ((), (), s32[]{:S(2)}) async-start(), calls=%async_computation.14 | async-start | bytes 7299072 | tf_op jit(solution)/shard_map/reduce_scatter | solution.py:273
  280.6 443.6 %reduce-scatter.8.cloned.1.call-start = ((), (), s32[]{:S(2)}) async-start(), calls=%async_computation.12 | async-start | bytes 7299072 | tf_op jit(solution)/shard_map/reduce_scatter | solution.py:271
  296.4 1.9 copy-start.7
  298.3 5.0 copy-start
  368.2 1.9 copy-start.7
  370.1 6.5 copy-start
  440.2 2.6 copy-start.19
  462.4 2.7 copy-start.23
  464.5 1.7 copy-start.5
  464.5 1.7 copy-start.31
  464.5 1.7 copy-start.35
  464.5 1.7 copy-start.37
  471.4 1.2 copy-start.24
  471.4 1.4 copy-start.26
  471.4 1.6 copy-start.28
  473.0 4.3 copy-start.41
  477.3 1.2 copy-start.13
  477.3 41.0 %copy-start.2 = (f32[512,768]{1,0:T(8,128)S(1)}, f32[512,768]{1,0:T(8,128)}, u32[]{:S(2)}) copy-start(f32[512,768]{1,0:T(8,128)} %copy-done.1) | copy-start | bytes 4718596
  477.3 40.9 %copy-start.9 = (bf16[512,768]{1,0:T(8,128)(2,1)S(1)}, bf16[512,768]{1,0:T(8,128)(2,1)}, u32[]{:S(2)}) copy-start(bf16[512,768]{1,0:T(8,128)(2,1)} %param.19) | copy-start | bytes 2359300
  477.3 40.9 %copy-start.39 = (f32[512]{0:T(512)S(1)}, f32[512]{0:T(512)}, u32[]{:S(2)}) copy-start(f32[512]{0:T(512)} %copy-done.38) | copy-start | bytes 6148
  518.2 3.2 copy-start.12
  518.2 3.2 copy-start.14
  518.3 3.2 copy-start.33
  518.3 3.2 copy-start.45
  (9 other events, 9.0 us)
Sparse Core Ops, SparseCore 0:
  10.9 62.7 all-gather.6
  76.6 52.7 all-gather.8
  132.2 58.8 all-gather.10
  193.8 54.2 all-gather.12
  269.0 98.8 reduce-scatter.9
  373.2 102.4 reduce-scatter.13
  481.3 118.5 reduce-scatter.11
  605.6 118.4 reduce-scatter.7
where the time goes:
time: 742 us; the launch traced here: 733 us
  waiting for transfers between devices  279 us (38%)
  matrix products  208 us (28%)
  blocking collectives  108 us (15%)
  local copies, waits for them, and re-layouts  72.7 us (10%)
  other arithmetic  47 us (6%)
  between operations  15.7 us (2%)
    reduce_scatter x1, waiting for transfers between devices, per_device(): lax.psum_scatter(qkv_term, ('tok', 'hd'), scatter_dimension=0, tiled=True)  123 us
    reduce_scatter x1, waiting for transfers between devices, per_device(): lax.psum_scatter(in_term, ('tok', 'hd'), scatter_dimension=0, tiled=True)  73.3 us
    dot_general x2, matrix products, one_block(): jnp.einsum('hqk,qhd->khd', grad_scores, query_block, preferred_element_ty...  59.3 us
    dot_general x2, matrix products, one_block(): jnp.einsum('hqk,khd->qhd', grad_scores, keys, preferred_element_type=jnp....  54.3 us
    all_gather x1, waiting for transfers between devices, per_device(): lax.all_gather(w_down, ('tok', 'hd'), axis=0, tiled=True)  50.2 us
    all_gather x1, blocking collectives, per_device(): lax.all_gather(norm_gains, ('tok', 'hd'), axis=1, tiled=True)  43.4 us
    unnamed x2, blocking collectives  40.3 us
    all_gather x1, waiting for transfers between devices, per_device(): lax.all_gather(w_in, ('tok', 'hd'), axis=0, tiled=True)  27.4 us
  transfers between devices with their start and end apart: 8, of which 5 were waited for; matrix products, arithmetic and copies ran while one was open for 40% of the time, Pallas kernels for 0%

commit v1 on v0

v1 whole, which is shorter than its diff:
```python
import functools
import math

import jax
import jax.numpy as jnp
import numpy as np
from jax import lax
from jax.experimental import pallas as pl
from jax.experimental.pallas import tpu as pltpu
from jax.sharding import PartitionSpec as P

HEADS = 12
HEAD_DIM = 64
EPS = 1e-05
THETA = 160000.0
NEG = -1e30
MESH = pl.DeviceIdType.MESH
F32 = jnp.float32
BF16 = jnp.bfloat16


def dot_nt(a, b):
    return lax.dot_general(a, b, (((1,), (1,)), ((), ())), preferred_element_type=F32)


def dot_nn(a, b):
    return lax.dot_general(a, b, (((1,), (0,)), ((), ())), preferred_element_type=F32)


def dot_tn(a, b):
    return lax.dot_general(a, b, (((0,), (0,)), ((), ())), preferred_element_type=F32)


def al(i, m):
    return pl.multiple_of(i, m)


def low_half(shape):
    lane = lax.broadcasted_iota(jnp.int32, shape, 1)
    return lane < HEAD_DIM


def rotated(u, cos, sin):
    lane = lax.broadcasted_iota(jnp.int32, cos.shape, 1)
    first = (lane % HEAD_DIM) < (HEAD_DIM // 2)
    parts = []
    for i in range(u.shape[1] // 128):
        s = u[:, i * 128 : (i + 1) * 128]
        swapped = jnp.where(first, pltpu.roll(s, 96, 1), pltpu.roll(s, 32, 1))
        parts.append(s * cos + swapped * sin)
    return parts[0] if len(parts) == 1 else jnp.concatenate(parts, axis=1)


def by_head(slab):
    lo = low_half(slab.shape)
    zero = jnp.zeros_like(slab)
    return jnp.where(lo, slab, zero), jnp.where(lo, zero, slab)


def norm_stats(u):
    mean = jnp.mean(u, axis=1, keepdims=True)
    centred = u - mean
    rstd = lax.rsqrt(jnp.mean(centred * centred, axis=1, keepdims=True) + EPS)
    return centred * rstd, rstd


def fold_rows(u):
    return jnp.sum(u.reshape(u.shape[0] // 8, 8, u.shape[1]), axis=0)


def layer_kernel(
    meta, x, cot, gains, wq, wo, wi, wd, freq,
    out, ingrad, gq, go, gi, gd, gg,
    x3, n1, cos_t, sin_t, krow, kcol, bias, q, k, v, p, att, res, n2, ga, gb, hid,
    cb, ggu, gres, gb1, gat, dkm, dsend, drecv, gqkv, gacc, pmeta,
    ssem, rsem,
):
    c = lax.axis_index("hd")
    half = x.shape[0] // 2
    rows = x.shape[0]
    d = x.shape[1]
    ff = wd.shape[1]
    so = al(c * half, half)
    mo = al((1 - c) * half, half)
    partner = {"hd": 1 - c}

    barrier = pltpu.get_barrier_semaphore()
    pl.semaphore_signal(barrier, inc=1, device_id=partner, device_id_type=MESH)
    pl.semaphore_wait(barrier, 1)

    def to_partner(src, dst, i):
        return pltpu.make_async_remote_copy(
            src, dst, ssem.at[i], rsem.at[i], device_id=partner, device_id_type=MESH
        )

    send_meta = to_partner(meta, pmeta, 0)
    send_x = to_partner(x.at[pl.ds(mo, half)], x3.at[pl.ds(2 * half, half)], 1)
    send_meta.start()
    send_x.start()
    x3[0:half] = x[pl.ds(so, half), :]
    x3[half : 2 * half] = x[pl.ds(mo, half), :]
    send_meta.wait()

    lane = lax.broadcasted_iota(jnp.int32, (1, half), 1)
    sets = ((meta, so, c * rows), (meta, mo, c * rows), (pmeta, so, (1 - c) * rows))
    for i, (ref, off, base) in enumerate(sets):
        cols = slice(i * half, (i + 1) * half)
        seg = ref[:, pl.ds(off, half)]
        local = lane + off
        grow = local + base
        valid = local < ref[0:1, rows : rows + 1]
        krow[0:1, cols] = jnp.where(valid, seg, -1 - grow).astype(F32)
        krow[1:2, cols] = seg.astype(F32)
        krow[2:3, cols] = grow.astype(F32)
        krow[3:8, cols] = jnp.broadcast_to(valid.astype(F32), (5, half))
    kcol[...] = krow[...].T

    def tables(i, _):
        r = pl.ds(al(i * 64, 64), 64)
        col = kcol[r, :]
        same = col[:, 1:2] == krow[1:2, :]
        start = jnp.min(jnp.where(same, krow[2:3, :], 1e9), axis=1, keepdims=True)
        angle = (col[:, 2:3] - start) * freq[0:1, :]
        cos_t[r, :] = jnp.cos(angle)
        sin_t[r, :] = jnp.sin(angle) * freq[1:2, :]
        return 0

    lax.fori_loop(0, 3 * half // 64, tables, 0)
    bias[:, 0:half] = jnp.where(kcol[0:half, 0:1] == krow[0:1, 0:half], 0.0, NEG)
    bias[:, half:] = jnp.where(kcol[half : 2 * half, 0:1] == krow[0:1, half:], 0.0, NEG)
    send_x.wait()

    def norm1(i, _):
        r = pl.ds(al(i * 128, 128), 128)
        n, _r = norm_stats(x3[r, :].astype(F32))
        n1[r, :] = (n * gains[0:1, :]).astype(BF16)
        return 0

    lax.fori_loop(0, 3 * half // 128, norm1, 0)

    def project(j, _):
        b = pl.ds(al(j * 256, 256), 256)
        u = dot_nt(n1[0:rows, :], wq[b, :])
        q[:, b] = (rotated(u, cos_t[0:rows, :], sin_t[0:rows, :]) * 0.125).astype(BF16)
        u = dot_nt(n1[...], wq[pl.ds(al(d + j * 256, 256), 256), :])
        k[:, b] = rotated(u, cos_t[...], sin_t[...]).astype(BF16)
        u = dot_nt(n1[...], wq[pl.ds(al(2 * d + j * 256, 256), 256), :])
        v[:, b] = u.astype(BF16)
        return 0

    lax.fori_loop(0, d // 256, project, 0)

    qs_, ks_ = (slice(0, half), slice(half, rows)), (slice(0, half), slice(half, 3 * half))

    def attend(hp, _):
        lanes = pl.ds(al(hp * 128, 128), 128)
        for qs, ks in zip(qs_, ks_):
            qh = by_head(q[qs, lanes])
            kk = k[ks, lanes]
            vh = by_head(v[ks, lanes])
            probs = []
            for h in range(2):
                s = dot_nt(qh[h], kk) + bias[:, ks]
                e = jnp.exp(s - jnp.max(s, axis=1, keepdims=True))
                e = (e * (1.0 / jnp.sum(e, axis=1, keepdims=True))).astype(BF16)
                p[2 * hp + h, :, ks] = e
                probs.append(e)
            o = dot_nn(jnp.concatenate(probs, axis=1), jnp.concatenate(vh, axis=0))
            att[qs, lanes] = o.astype(BF16)
        return 0

    lax.fori_loop(0, HEADS // 2, attend, 0)

    def after_attention(i, _):
        r = pl.ds(al(i * 256, 256), 256)
        u = x3[r, :].astype(F32) + kcol[r, 3:4] * dot_nt(att[r, :], wo[...])
        res[r, :] = u
        n, _r = norm_stats(u)
        n2[r, :] = (n * gains[1:2, :]).astype(BF16)
        return 0

    lax.fori_loop(0, rows // 256, after_attention, 0)

    def feed(j, _):
        b = pl.ds(al(j * 128, 128), 128)
        w = jnp.concatenate([wi[b, :], wi[pl.ds(al(ff + j * 128, 128), 128), :]], axis=0)
        u = dot_nt(n2[...], w)
        gate, up = u[:, :128], u[:, 128:]
        cdf = 0.5 * (1.0 + lax.erf(gate * (1.0 / math.sqrt(2.0))))
        pdf = jnp.exp(-0.5 * gate * gate) * (1.0 / math.sqrt(2.0 * math.pi))
        act = gate * cdf
        ga[:, b] = up * (cdf + gate * pdf)
        gb[:, b] = act
        hid[:, b] = (act * up).astype(BF16)
        return 0

    lax.fori_loop(0, ff // 128, feed, 0)

    for i, off in ((0, so), (1, mo)):
        r = slice(i * half, (i + 1) * half)
        cb[r, :] = (cot[pl.ds(off, half), :].astype(F32) * kcol[r, 3:4]).astype(BF16)

    def down(j, _):
        b = pl.ds(al(j * 256, 256), 256)
        y = (res[:, b] + kcol[0:rows, 3:4] * dot_nt(hid[...], wd[b, :])).astype(BF16)
        out[pl.ds(so, half), b] = y[:half]
        out[pl.ds(mo, half), b] = y[half:]
        return 0

    lax.fori_loop(0, d // 256, down, 0)

    def down_grad(j, _):
        b = pl.ds(al(j * 256, 256), 256)
        gd[b, :] = dot_tn(cb[:, b], hid[...]).astype(gd.dtype)
        return 0

    lax.fori_loop(0, d // 256, down_grad, 0)

    def hidden_grad(j, _):
        b = pl.ds(al(j * 384, 384), 384)
        u = dot_nn(cb[...], wd[:, b])
        ggu[:, b] = (u * ga[:, b]).astype(BF16)
        ggu[:, pl.ds(al(ff + j * 384, 384), 384)] = (u * gb[:, b]).astype(BF16)
        return 0

    lax.fori_loop(0, ff // 384, hidden_grad, 0)
    gacc[...] = jnp.zeros_like(gacc)

    def feed_back(i, _):
        r = pl.ds(al(i * 256, 256), 256)
        off = al(jnp.where(i == 0, so, mo), 256)
        g = dot_nn(ggu[r, :], wi[...])
        n, rstd = norm_stats(res[r, :])
        gacc[8:16, :] += fold_rows(g * n)
        g = g * gains[1:2, :]
        g = g - jnp.mean(g, axis=1, keepdims=True) - n * jnp.mean(g * n, axis=1, keepdims=True)
        g = cot[pl.ds(off, 256), :].astype(F32) + rstd * g
        gres[r, :] = g
        gb1[r, :] = (g * kcol[r, 3:4]).astype(BF16)
        return 0

    lax.fori_loop(0, rows // 256, feed_back, 0)

    def in_grad(j, _):
        b = pl.ds(al(j * 256, 256), 256)
        gi[b, :] = dot_tn(ggu[:, b], n2[...]).astype(gi.dtype)
        return 0

    lax.fori_loop(0, 2 * ff // 256, in_grad, 0)

    def out_grad(j, _):
        b = pl.ds(al(j * 256, 256), 256)
        go[b, :] = dot_tn(gb1[:, b], att[...]).astype(go.dtype)
        gat[:, b] = dot_nn(gb1[...], wo[:, b]).astype(BF16)
        return 0

    lax.fori_loop(0, d // 256, out_grad, 0)

    def attend_back(hp, qs, ks):
        lanes = pl.ds(al(hp * 128, 128), 128)
        do = gat[qs, lanes]
        doh = by_head(do)
        qh = by_head(q[qs, lanes])
        kh = by_head(k[ks, lanes])
        vv = v[ks, lanes]
        deltas = by_head(do.astype(F32) * att[qs, lanes].astype(F32))
        ds, ps = [], []
        for h in range(2):
            delta = jnp.sum(deltas[h], axis=1, keepdims=True)
            ph = p[2 * hp + h, :, ks]
            dp = dot_nt(doh[h], vv)
            ds.append((ph.astype(F32) * (dp - delta)).astype(BF16))
            ps.append(ph)
        dq = dot_nn(jnp.concatenate(ds, axis=1), jnp.concatenate(kh, axis=0)) * 0.125
        dk = dot_tn(jnp.concatenate(ds, axis=0), jnp.concatenate(qh, axis=0))
        dv = dot_tn(jnp.concatenate(ps, axis=0), jnp.concatenate(doh, axis=0))
        gqkv[qs, lanes] = rotated(dq, cos_t[qs, :], -sin_t[qs, :]).astype(BF16)
        return dk, dv

    def back_shared(hp, _):
        dk, dv = attend_back(hp, qs_[1], ks_[1])
        a, b = pl.ds(al(hp * 128, 128), 128), pl.ds(al(d + hp * 128, 128), 128)
        dkm[:, a] = dk[:half]
        dkm[:, b] = dv[:half]
        dsend[:, a] = dk[half:].astype(BF16)
        dsend[:, b] = dv[half:].astype(BF16)
        return 0

    lax.fori_loop(0, HEADS // 2, back_shared, 0)
    send_d = to_partner(dsend, drecv, 2)
    send_d.start()

    def back_solo(hp, _):
        dk, dv = attend_back(hp, qs_[0], ks_[0])
        a, b = pl.ds(al(d + hp * 128, 128), 128), pl.ds(al(2 * d + hp * 128, 128), 128)
        gqkv[0:half, a] = rotated(dk, cos_t[0:half, :], -sin_t[0:half, :]).astype(BF16)
        gqkv[0:half, b] = dv.astype(BF16)
        return 0

    lax.fori_loop(0, HEADS // 2, back_solo, 0)
    send_d.wait()

    def join(hp, _):
        a, b = pl.ds(al(hp * 128, 128), 128), pl.ds(al(d + hp * 128, 128), 128)
        e = pl.ds(al(2 * d + hp * 128, 128), 128)
        dk = dkm[:, a] + drecv[:, a].astype(F32)
        dv = dkm[:, b] + drecv[:, b].astype(F32)
        r = slice(half, rows)
        gqkv[r, b] = rotated(dk, cos_t[r, :], -sin_t[r, :]).astype(BF16)
        gqkv[r, e] = dv.astype(BF16)
        return 0

    lax.fori_loop(0, HEADS // 2, join, 0)

    def qkv_grad(j, _):
        b = pl.ds(al(j * 256, 256), 256)
        gq[b, :] = dot_tn(gqkv[:, b], n1[0:rows, :]).astype(gq.dtype)
        return 0

    lax.fori_loop(0, 3 * d // 256, qkv_grad, 0)

    def first_back(i, _):
        r = pl.ds(al(i * 256, 256), 256)
        off = al(jnp.where(i == 0, so, mo), 256)
        g = dot_nn(gqkv[r, :], wq[...])
        n, rstd = norm_stats(x3[r, :].astype(F32))
        gacc[0:8, :] += fold_rows(g * n)
        g = g * gains[0:1, :]
        g = g - jnp.mean(g, axis=1, keepdims=True) - n * jnp.mean(g * n, axis=1, keepdims=True)
        ingrad[pl.ds(off, 256), :] = (gres[r, :] + rstd * g).astype(BF16)
        return 0

    lax.fori_loop(0, rows // 256, first_back, 0)
    gg[0:1, :] = jnp.sum(gacc[0:8, :], axis=0, keepdims=True)
    gg[1:2, :] = jnp.sum(gacc[8:16, :], axis=0, keepdims=True)


def frequency_rows():
    w = np.arange(128) % HEAD_DIM
    f = np.float32(THETA) ** (-(w % 32).astype(np.float32) * 2.0 / HEAD_DIM)
    sign = np.where(w < 32, -1.0, 1.0)
    rows = np.zeros((8, 128), np.float32)
    rows[0], rows[1] = f, sign
    return rows


def per_device(
    hidden_in, norm_gains, w_qkv, w_attn_out, w_in, w_down, cotangent, segment_ids, row_counts
):
    both = ("tok", "hd")
    rows, d = hidden_in.shape
    ff = w_down.shape[1]
    half = rows // 2
    wq, wo, wi, wd = (
        lax.all_gather(w, both, axis=0, tiled=True) for w in (w_qkv, w_attn_out, w_in, w_down)
    )
    gains = lax.all_gather(norm_gains, both, axis=1, tiled=True).astype(F32)
    meta = jnp.concatenate([segment_ids, jnp.broadcast_to(row_counts, (128,))])[None]
    vmem = pl.BlockSpec(memory_space=pltpu.VMEM)
    V = pltpu.VMEM
    gdt = BF16
    outs = pl.pallas_call(
        layer_kernel,
        out_shape=[
            jax.ShapeDtypeStruct((rows, d), BF16),
            jax.ShapeDtypeStruct((rows, d), BF16),
            jax.ShapeDtypeStruct((3 * d, d), gdt),
            jax.ShapeDtypeStruct((d, d), gdt),
            jax.ShapeDtypeStruct((2 * ff, d), gdt),
            jax.ShapeDtypeStruct((d, ff), gdt),
            jax.ShapeDtypeStruct((2, d), F32),
        ],
        in_specs=[vmem] * 9,
        out_specs=[vmem] * 7,
        scratch_shapes=[
            V((3 * half, d), BF16),
            V((3 * half, d), BF16),
            V((3 * half, 128), F32),
            V((3 * half, 128), F32),
            V((8, 3 * half), F32),
            V((3 * half, 8), F32),
            V((half, 3 * half), F32),
            V((rows, d), BF16),
            V((3 * half, d), BF16),
            V((3 * half, d), BF16),
            V((HEADS, half, 3 * half), BF16),
            V((rows, d), BF16),
            V((rows, d), F32),
            V((rows, d), BF16),
            V((rows, ff), F32),
            V((rows, ff), F32),
            V((rows, ff), BF16),
            V((rows, d), BF16),
            V((rows, 2 * ff), BF16),
            V((rows, d), F32),
            V((rows, d), BF16),
            V((rows, d), BF16),
            V((half, 2 * d), F32),
            V((half, 2 * d), BF16),
            V((half, 2 * d), BF16),
            V((rows, 3 * d), BF16),
            V((16, d), F32),
            V(meta.shape, jnp.int32),
            pltpu.SemaphoreType.DMA((3,)),
            pltpu.SemaphoreType.DMA((3,)),
        ],
        compiler_params=pltpu.CompilerParams(
            collective_id=0, has_side_effects=True, vmem_limit_bytes=67043328
        ),
    )(meta, hidden_in, cotangent, gains, wq, wo, wi, wd, jnp.asarray(frequency_rows()))
    output, input_grad, gq, go, gi, gd, gg = outs
    total = rows * lax.axis_size("tok") * lax.axis_size("hd")
    scale = 1.0 / math.sqrt(total)
    sums = [
        lax.psum_scatter(g, both, scatter_dimension=0, tiled=True).astype(F32) * scale
        for g in (gq, go, gi, gd)
    ]
    sum_g = lax.psum_scatter(gg, both, scatter_dimension=1, tiled=True) * scale
    return (output, input_grad, *sums, sum_g)


def solution(mesh):
    both = ("tok", "hd")
    return jax.shard_map(
        per_device,
        mesh=mesh,
        in_specs=(
            P(both, None), P(None, both), P(both, None), P(both, None), P(both, None),
            P(both, None), P(both, None), P(both), P(both),
        ),
        out_specs=(
            P(both, None), P(both, None), P(both, None), P(both, None), P(both, None),
            P(both, None), P(None, both),
        ),
        check_vma=False,
    )
```

time: 742 us -> 724 us (0.976); the launches traced: 733 us -> 723 us
  waiting for transfers between devices: 279 us -> 556 us
  matrix products: 208 us -> 0 us
  local copies, waits for them, and re-layouts: 72.7 us -> 3.91 us
  Pallas kernels: 0 us -> 59.6 us
  other arithmetic: 47 us -> 6.7 us
  blocking collectives: 108 us -> 82 us
    dot_general x26 -> x0, matrix products: 208 us -> none  [the longest x2 59.3 us: one_block(): jnp.einsum('hqk,qhd->khd', grad_scores, query_block, preferred_element_ty...]
    all_gather x4, waiting for transfers between devices: 80.1 us -> 192 us  [per_device(): lax.all_gather(w, both, axis=0, tiled=True)]
    unnamed x9, waiting for transfers between devices: 2.65 us -> 96.6 us
    reduce_scatter x3, waiting for transfers between devices: 196 us -> 267 us  [per_device(): lax.psum_scatter(g, both, scatter_dimension=0, tiled=True).astype(F32)]
    pallas_call x0 -> x1, Pallas kernels: none -> 59.6 us  [per_device(): pl.pallas_call(layer_kernel, out_shape=[jax.ShapeDtypeStruct((rows, d), B...]
    all_to_all x4 -> x0, blocking collectives: 22.3 us -> none  [the longest x1 6.26 us: per_device(): lax.all_to_all(grad_stack, 'hd', split_axis=0, concat_axis=2, tiled=True)]
    unnamed x98 -> x8, local copies, waits for them, and re-layouts: 22.2 us -> 1.77 us
    reduce_sum x7 -> x0, other arithmetic: 11.8 us -> none  [the longest x2 7.27 us: one_block(): total = jnp.sum(weights_exp, axis=-1, keepdims=True)]
  transfers between devices with their start and end apart: 8 -> 8, of which waited for: 5 -> 8; matrix products, arithmetic and copies ran while one was open for 40% -> 1% of each run, Pallas kernels for 0% -> 0%
where the time goes in v1:
time: 724 us; the launch traced here: 723 us
  waiting for transfers between devices  556 us (77%)
  blocking collectives  82 us (11%)
  Pallas kernels  59.6 us (8%)
  between operations  14.8 us (2%)
    reduce_scatter x3, waiting for transfers between devices, per_device(): lax.psum_scatter(g, both, scatter_dimension=0, tiled=True).astype(F32)  267 us
    all_gather x4, waiting for transfers between devices, per_device(): lax.all_gather(w, both, axis=0, tiled=True)  192 us
    unnamed x9, waiting for transfers between devices  96.6 us
    pallas_call x1, Pallas kernels, per_device(): pl.pallas_call(layer_kernel, out_shape=[jax.ShapeDtypeStruct((rows, d), B...  59.6 us
    all_gather x1, blocking collectives, per_device(): gains = lax.all_gather(norm_gains, both, axis=1, tiled=True).astype(F32)  43.5 us
    unnamed x1, blocking collectives  38.6 us
  transfers between devices with their start and end apart: 8, of which 8 were waited for; matrix products, arithmetic and copies ran while one was open for 1% of the time, Pallas kernels for 0%

profile of v1, /device:TPU:0, one launch (start us, length us, event | category | flops | bytes accessed | tf_op | source)
XLA Modules:
  0.0 723.4 jit_solution(10706674954724832949)
XLA Ops:
  7.2 0.0 all-gather.8.cloned.1.call-start
  7.2 0.7 all-gather.8.cloned.1.call-update
  7.9 0.0 all-gather.12.cloned.1.call-start
  7.9 0.7 all-gather.12.cloned.1.call-update
  8.7 0.0 all-gather.10.cloned.1.call-start
  8.7 0.7 all-gather.10.cloned.1.call-update
  9.4 0.0 all-gather.6.cloned.1.call-start
  9.4 0.5 all-gather.6.cloned.1.call-update
  10.0 0.0 reduce-scatter.10.cloned.1.call-start
  10.0 43.5 %all-gather = bf16[32,24,2]{1,2,0:T(2,128)(2,1)S(1)} all-gather(bf16[1,24,2]{1,2,0:T(2,128)(2,1)} %bitcast.11), channel_id=1, replica_groups=mesh['tok'=16,'hd'=2] {'tok','hd'}, dimensions={0}, use_global_device_ids=true | all-gather | bytes 3168 | tf_op jit(solution)/shard_map/all_gather | solution.py:357
  53.5 0.1 copy.20
  53.6 0.1 copy.21
  53.6 0.7 reshape.16
  55.0 0.7 concatenate.3
  55.7 0.6 broadcast_in_dim.9.meta
  56.3 11.3 %all-gather.8.cloned.1.call-done.wo = bf16[768,768]{1,0:T(8,128)(2,1)} async-done(((bf16[24,768]{1,0:T(8,128)(2,1)}), bf16[768,768]{1,0:T(8,128)(2,1)}) %all-gather.8.cloned.1.call-update) | async-done | bytes 1179664 | tf_op jit(solution)/shard_map/all_gather | solution.py:355
  67.6 57.2 %all-gather.12.cloned.1.call-done.wd = bf16[768,1152]{1,0:T(8,128)(2,1)} async-done(((bf16[24,1152]{1,0:T(8,128)(2,1)}), bf16[768,1152]{1,0:T(8,128)(2,1)}) %all-gather.12.cloned.1.call-update) | async-done | bytes 1769488 | tf_op jit(solution)/shard_map/all_gather | solution.py:355
  124.8 61.9 %all-gather.10.cloned.1.call-done.wi = bf16[2304,768]{1,0:T(8,128)(2,1)} async-done(((bf16[72,768]{1,0:T(8,128)(2,1)}), bf16[2304,768]{1,0:T(8,128)(2,1)}) %all-gather.10.cloned.1.call-update) | async-done | bytes 3538960 | tf_op jit(solution)/shard_map/all_gather | solution.py:355
  186.7 61.6 %all-gather.6.cloned.1.call-done.wq = bf16[2304,768]{1,0:T(8,128)(2,1)} async-done(((bf16[72,768]{1,0:T(8,128)(2,1)}), bf16[2304,768]{1,0:T(8,128)(2,1)}) %all-gather.6.cloned.1.call-update) | async-done | bytes 3538960 | tf_op jit(solution)/shard_map/all_gather | solution.py:355
  248.3 59.6 %shard_map.153 = (bf16[512,768]{1,0:T(8,128)(2,1)}, bf16[512,768]{1,0:T(8,128)(2,1)}, bf16[2304,768]{1,0:T(8,128)(2,1)}, bf16[768,768]{1,0:T(8,128)(2,1)}, bf16[...) custom-call(s32[1,640]{1,0:T(1,128)} %broadcast_in_dim.9.meta, bf16[512,768]{1,0:T(8,128)(2,1)} %x.3, ...), custom_call_target="tpu_custom_call" | custom-call | tf_op jit(solution)/shard_map/pallas_call | solution.py:362
  307.9 0.0 reduce-scatter.10.cloned.1.call-update
  308.0 0.0 reduce-scatter.14.cloned.1.call-start
  308.0 0.5 reduce-scatter.14.cloned.1.call-update
  308.5 0.0 reduce-scatter.12.cloned.1.call-start
  308.6 0.0 copy-start.2
  308.6 0.0 copy-start.1
  308.6 0.7 reduce-scatter.12.cloned.1.call-update
  309.3 0.0 copy-start
  309.3 0.0 reduce-scatter.8.cloned.1.call-start
  309.3 0.7 reduce-scatter.8.cloned.1.call-update
  310.1 0.0 copy-done.2
  310.1 38.6 %all-reduce.2 = f32[2,768]{1,0:T(2,128)S(1)} all-reduce(f32[2,768]{1,0:T(2,128)S(1)} %copy-done.2), channel_id=6, replica_groups=mesh['tok'=16,'hd'=2] {'tok','hd'}, use_global_device_ids=true, to_apply=%region_4.0.clone | all-reduce | flops 1536 | bytes 12288
  348.6 0.6 dynamic-slice_multiply_fusion
  349.3 54.7 %reduce-scatter.10.cloned.1.call-done = bf16[24,768]{1,0:T(8,128)(2,1)} async-done(((bf16[768,768]{1,0:T(8,128)(2,1)}), bf16[24,768]{1,0:T(8,128)(2,1)}) %reduce-scatter.10.cloned.1.call-update) | async-done | bytes 36880 | tf_op jit(solution)/shard_map/reduce_scatter | solution.py:415
  403.9 1.4 convert_multiply_fusion.3
  405.3 92.1 %reduce-scatter.14.cloned.1.call-done = bf16[24,1152]{1,0:T(8,128)(2,1)} async-done(((bf16[768,1152]{1,0:T(8,128)(2,1)}), bf16[24,1152]{1,0:T(8,128)(2,1)}) %reduce-scatter.14.cloned.1.call-update) | async-done | bytes 55312
  497.4 1.5 convert_multiply_fusion.2
  498.9 106.5 %reduce-scatter.12.cloned.1.call-done = bf16[72,768]{1,0:T(8,128)(2,1)} async-done(((bf16[2304,768]{1,0:T(8,128)(2,1)}), bf16[72,768]{1,0:T(8,128)(2,1)}) %reduce-scatter.12.cloned.1.call-update) | async-done | bytes 110608 | tf_op jit(solution)/shard_map/reduce_scatter | solution.py:415
  605.4 1.6 convert_multiply_fusion
  607.0 106.2 %reduce-scatter.8.cloned.1.call-done = bf16[72,768]{1,0:T(8,128)(2,1)} async-done(((bf16[2304,768]{1,0:T(8,128)(2,1)}), bf16[72,768]{1,0:T(8,128)(2,1)}) %reduce-scatter.8.cloned.1.call-update) | async-done | bytes 110608 | tf_op jit(solution)/shard_map/reduce_scatter | solution.py:415
  713.2 1.6 convert_multiply_fusion.1
  714.8 0.0 copy-done.1
  714.8 0.9 copy.27
  715.7 0.0 copy-done
  715.7 0.9 copy.28
Async XLA Ops:
  7.2 60.4 %all-gather.8.cloned.1.call-start = ((), (), s32[]{:S(2)}) async-start(), calls=%async_computation.5 | async-start | bytes 1216512 | tf_op jit(solution)/shard_map/all_gather | solution.py:355
  7.9 116.9 %all-gather.12.cloned.1.call-start = ((), (), s32[]{:S(2)}) async-start(), calls=%async_computation.7 | async-start | bytes 1824768 | tf_op jit(solution)/shard_map/all_gather | solution.py:355
  8.7 178.0 %all-gather.10.cloned.1.call-start = ((), (), s32[]{:S(2)}) async-start(), calls=%async_computation.6 | async-start | bytes 3649536 | tf_op jit(solution)/shard_map/all_gather | solution.py:355
  9.4 238.9 %all-gather.6.cloned.1.call-start = ((), (), s32[]{:S(2)}) async-start(), calls=%async_computation.4 | async-start | bytes 3649536 | tf_op jit(solution)/shard_map/all_gather | solution.py:355
  10.0 394.0 %reduce-scatter.10.cloned.1.call-start = ((), (), s32[]{:S(2)}) async-start(), calls=%async_computation.9 | async-start | bytes 1216512 | tf_op jit(solution)/shard_map/reduce_scatter | solution.py:415
  308.0 189.5 %reduce-scatter.14.cloned.1.call-start = ((), (), s32[]{:S(2)}) async-start(), calls=%async_computation.11 | async-start | bytes 1824768
  308.5 296.8 %reduce-scatter.12.cloned.1.call-start = ((), (), s32[]{:S(2)}) async-start(), calls=%async_computation.10 | async-start | bytes 3649536 | tf_op jit(solution)/shard_map/reduce_scatter | solution.py:415
  308.6 1.5 copy-start.2
  308.6 406.2 %copy-start.1 = (bf16[512,768]{1,0:T(8,128)(2,1)S(1)}, bf16[512,768]{1,0:T(8,128)(2,1)}, u32[]{:S(2)}) copy-start(bf16[512,768]{1,0:T(8,128)(2,1)} %get-tuple-element.28) | copy-start | bytes 2359300
  309.3 406.4 %copy-start = (bf16[512,768]{1,0:T(8,128)(2,1)S(1)}, bf16[512,768]{1,0:T(8,128)(2,1)}, u32[]{:S(2)}) copy-start(bf16[512,768]{1,0:T(8,128)(2,1)} %get-tuple-element.29) | copy-start | bytes 2359300
  309.3 403.9 %reduce-scatter.8.cloned.1.call-start = ((), (), s32[]{:S(2)}) async-start(), calls=%async_computation.8 | async-start | bytes 3649536 | tf_op jit(solution)/shard_map/reduce_scatter | solution.py:415
Sparse Core Ops, SparseCore 0:
  10.9 56.6 all-gather.7
  70.4 54.3 all-gather.11
  127.7 58.9 all-gather.9
  189.4 58.7 all-gather.5
  308.1 95.8 reduce-scatter.9
  409.1 88.2 reduce-scatter.13
  502.8 102.4 reduce-scatter.11
  610.8 102.3 reduce-scatter.7
